TPU v7x, 32 devices: a whole 2x2x4 slice. The times are simulated.
32 devices in a mesh: ctx: 4 (over z), fsdp: 2 (over core), kvh: 4 (over y, x).
Axes of the slice: x: 2, y: 2, z: 4, core: 2. Of those that a mesh axis runs over, the one named last changes fastest.
Arguments:
- hidden: bfloat16 [2048, 4096], P(('ctx', 'fsdp'), 'kvh'), may hold values from -6 to 6
- key_value_matrix: bfloat16 [4096, 2048], P('fsdp', 'kvh'), may hold values from -0.09375 to 0.09375
- queries: bfloat16 [2048, 4096], P(('ctx', 'fsdp'), 'kvh')
- vertical_blocks: int32 [8, 8], P('kvh'), may hold values from 0 to 15, as said below
- slash_offsets: int32 [8, 2], P('kvh'), may hold values from 1 to 15, as said below
Outputs:
- attended: bfloat16 [2048, 4096], P(('ctx', 'fsdp'), 'kvh')
Inputs may be any that keep to these rules, and one draw needn't show every extreme that they name: `vertical_blocks`: the 8 entries of one head are distinct key blocks. `slash_offsets`: the 2 entries of one head are distinct block distances.
All inputs are finite; a program needn't handle non-finite values.
Results may differ from a plain program's by a relative error of at most 0.012.
The roundings to bfloat16 on the way count: a program that leaves them out, or rounds other values in their place, can miss the bound.
Values may be sent and summed in bfloat16 or wider, within the bound.
No kernel may reach another device: no remote copies, remote signals or barrier semaphores. Data moves between devices by JAX's collectives and lax.ppermute only.
A program may use at most 64 MiB of HBM per device.

v0:
```python
import jax
import jax.numpy as jnp
from jax import lax
from jax.sharding import PartitionSpec as P

HEAD_DIMENSION = 128
BLOCK_TOKENS = 128


def broadcast(value, axis, source):
    kept = jnp.where(lax.axis_index(axis) == source, value, 0).astype(value.dtype)
    return lax.psum(kept, axis)


def from_behind(value, axis, by):
    size = lax.axis_size(axis)
    pairs = [(i, i + by) for i in range(size) if 0 <= i + by < size]
    return lax.ppermute(value, axis, pairs)


def rotate_keys(raw_keys, positions):
    half = raw_keys.shape[-1] // 2
    frequency = jnp.power(
        500000.0, -(jnp.arange(half, dtype=jnp.float32) * 2.0 / raw_keys.shape[-1])
    )
    angle = positions[:, None] * frequency[None, :]
    cosine = jnp.cos(angle)[:, None, :]
    sine = jnp.sin(angle)[:, None, :]
    first_half = raw_keys[..., :half]
    second_half = raw_keys[..., half:]
    return jnp.concatenate(
        [first_half * cosine - second_half * sine, second_half * cosine + first_half * sine],
        axis=-1,
    )


def per_device(hidden, key_value_matrix, queries, vertical_blocks, slash_offsets):
    tok_rows = hidden.shape[0]
    head_size = HEAD_DIMENSION
    block_rows = BLOCK_TOKENS
    local_count = tok_rows // block_rows
    local_heads = key_value_matrix.shape[1] // (2 * head_size)
    gathered = lax.all_gather(hidden, "kvh", axis=1, tiled=True)
    projected_tokens = jnp.dot(
        gathered,
        lax.all_gather(key_value_matrix, "fsdp", axis=0, tiled=True),
        preferred_element_type=jnp.float32,
    )
    projected_tokens = projected_tokens.reshape(tok_rows, local_heads, 2, head_size)
    position = lax.axis_index(("ctx", "fsdp"))
    positions = (position * tok_rows + jnp.arange(tok_rows, dtype=jnp.int32)).astype(jnp.float32)
    key_tensor = rotate_keys(projected_tokens[:, :, 0], positions).astype(jnp.bfloat16)
    value_tensor = projected_tokens[:, :, 1].astype(jnp.bfloat16)
    own_blocks = (
        jnp.stack([key_tensor, value_tensor], axis=2)
        .reshape(local_count, block_rows, local_heads, 2, head_size)
        .transpose(2, 0, 1, 3, 4)
    )
    shards = lax.axis_size(("ctx", "fsdp"))
    vertical_count = vertical_blocks.shape[1]
    slash_count = slash_offsets.shape[1]

    def fetch_block(counter, buffer):
        head_index = counter // vertical_count
        slot_index = counter % vertical_count
        wanted = vertical_blocks[head_index, slot_index]
        head_blocks = lax.dynamic_index_in_dim(own_blocks, head_index, 0, keepdims=False)
        outgoing = lax.dynamic_index_in_dim(head_blocks, wanted % local_count, 0, keepdims=False)
        received = broadcast(outgoing, ("ctx", "fsdp"), wanted // local_count)
        return buffer.at[head_index, slot_index].set(received)

    start_buffer = jnp.zeros((local_heads, vertical_count) + own_blocks.shape[2:], jnp.bfloat16)
    vertical_kv = lax.fori_loop(0, local_heads * vertical_count, fetch_block, start_buffer)
    device_shift = slash_offsets // local_count
    remainder = slash_offsets % local_count
    moving = jnp.broadcast_to(
        own_blocks[:, None], (local_heads, slash_count) + own_blocks.shape[1:]
    )
    for digit in range((shards - 1).bit_length()):
        shifted = from_behind(moving, ("ctx", "fsdp"), 1 << digit)
        chosen = device_shift // (1 << digit) % 2 == 1
        moving = jnp.where(chosen[:, :, None, None, None, None], shifted, moving)
    earlier = from_behind(moving, ("ctx", "fsdp"), 1)
    extended = jnp.concatenate([earlier, moving], axis=2)
    local_ids = jnp.arange(local_count, dtype=jnp.int32)
    wanted_index = local_count + local_ids[None, None, :] - remainder[:, :, None]
    selector = (wanted_index[..., None] == jnp.arange(2 * local_count, dtype=jnp.int32)).astype(
        jnp.bfloat16
    )
    slash_kv = jnp.einsum(
        "hnbk,hnkucd->hnbucd", selector, extended, preferred_element_type=jnp.float32
    ).astype(jnp.bfloat16)
    slot_ids = jnp.arange(1 + vertical_count + slash_count, dtype=jnp.int32)
    token_ids = jnp.arange(block_rows, dtype=jnp.int32)
    token_ok = (slot_ids[None, :, None] > 0) | (
        token_ids[None, None, :] <= token_ids[:, None, None]
    )
    group_size = queries.shape[1] // (local_heads * head_size)
    query_blocks = queries.reshape(local_count, block_rows, local_heads, group_size, head_size)
    scale = head_size ** (-0.5)

    def attend(item):
        own_one, slash_one, query_one, local_index = item
        mask_block = position * local_count + local_index
        all_blocks = jnp.concatenate([own_one[:, None], vertical_kv, slash_one], axis=1)
        key_sel = all_blocks[:, :, :, 0]
        value_sel = all_blocks[:, :, :, 1]
        vertical_allowed = (vertical_blocks < mask_block) & jnp.logical_not(
            jnp.any(
                (mask_block - vertical_blocks)[:, :, None] == slash_offsets[:, None, :], axis=-1
            )
        )
        slash_allowed = slash_offsets <= mask_block
        valid_mask = jnp.concatenate(
            [jnp.ones((local_heads, 1), dtype=bool), vertical_allowed, slash_allowed], axis=1
        )
        allowed = valid_mask[:, None, None, :, None] & token_ok[None, None]
        scores = (
            jnp.einsum("thgd,hsud->hgtsu", query_one, key_sel, preferred_element_type=jnp.float32)
            * scale
        )
        scores = jnp.where(allowed, scores, -jnp.inf)
        largest = jnp.max(scores, axis=(3, 4), keepdims=True)
        expo = jnp.exp(scores - largest)
        probs = (expo / jnp.sum(expo, axis=(3, 4), keepdims=True)).astype(jnp.bfloat16)
        result = jnp.einsum(
            "hgtsu,hsud->thgd", probs, value_sel, preferred_element_type=jnp.float32
        )
        return result.astype(jnp.bfloat16).reshape(block_rows, local_heads * group_size * head_size)

    inputs = (
        own_blocks.transpose(1, 0, 2, 3, 4),
        slash_kv.transpose(2, 0, 1, 3, 4, 5),
        query_blocks,
        local_ids,
    )
    outputs = lax.map(attend, inputs)
    return outputs.reshape(tok_rows, local_heads * group_size * head_size)


def solution(mesh):
    return jax.shard_map(
        per_device,
        mesh=mesh,
        in_specs=(
            P(("ctx", "fsdp"), "kvh"),
            P("fsdp", "kvh"),
            P(("ctx", "fsdp"), "kvh"),
            P("kvh", None),
            P("kvh", None),
        ),
        out_specs=P(("ctx", "fsdp"), "kvh"),
        check_vma=False,
    )
```

profile of v0, /device:TPU:0, one launch (start us, length us, event | category | flops | bytes accessed | tf_op | source)
XLA Modules:
  0.0 1108.5 jit_solution(16996056453087566824)
XLA Ops:
  8.4 38.8 %all-gather.3.cloned.1.call-done = bf16[256,4096]{1,0:T(8,128)(2,1)} async-done(((bf16[256,1024]{1,0:T(8,128)(2,1)}), bf16[256,4096]{1,0:T(8,128)(2,1)}) %all-gather.3.cloned.1.call-update) | async-done | bytes 2097168 | tf_op jit(solution)/shard_map/all_gather | solution.py:43
  47.1 15.2 %all-gather.5.cloned.1.call-done = bf16[4096,512]{1,0:T(8,128)(2,1)} async-done(((bf16[2048,512]{1,0:T(8,128)(2,1)}), bf16[4096,512]{1,0:T(8,128)(2,1)}) %all-gather.5.cloned.1.call-update) | async-done | bytes 4194320 | tf_op jit(solution)/shard_map/all_gather | solution.py:46
  62.4 4.1 fusion.22
  68.7 2.2 collective-permute-start
  70.9 1.4 collective-permute-done
  73.0 10.5 collective-permute-start.1
  83.6 10.4 collective-permute-done.1
  94.8 5.3 collective-permute-start.2
  100.6 9.2 collective-permute-done.2
  110.4 2.1 collective-permute-start.3
  113.5 2.4 fusion.10
  116.3 971.2 %while.30 = (s32[]{:T(128)}, bf16[2,8,128,2,128]{4,2,1,0,3:T(8,128)(2,1)S(1)}, s32[2,8]{1,0:T(2,128)S(1)}, bf16[2,2,128,2,128]{4,3,2,1,0:T(2,128)(2,1)S(1)}, s32...) while((s32[]{:T(128)}, ...), condition=%wide.region_3.4_spmd, body=%wide.region_0.3_spmd.sunk | while | flops 98376 | bytes 983881 | solution.py:73
  121.0 72.3 %all-reduce.2.cloned.1.call-done = bf16[1,1,128,2,128]{4,3,2,1,0:T(2,128)(2,1)} async-done(((bf16[1,1,128,2,128]{4,3,2,1,0:T(2,128)(2,1)}), bf16[1,1,128,2,128]{4,3,2,1,0:T(2,128)(2,1)}) %all-reduce.2.cloned.1.call-update) | async-done | bytes 65552 | tf_op jit(solution)/shard_map/while/body/eval_jaxpr/psum | solution.py:12
  193.4 1.6 broadcast_select_fusion.8
  199.7 53.2 %all-reduce.2.cloned.1.call-done = bf16[1,1,128,2,128]{4,3,2,1,0:T(2,128)(2,1)} async-done(((bf16[1,1,128,2,128]{4,3,2,1,0:T(2,128)(2,1)}), bf16[1,1,128,2,128]{4,3,2,1,0:T(2,128)(2,1)}) %all-reduce.2.cloned.1.call-update) | async-done | bytes 65552 | tf_op jit(solution)/shard_map/while/body/eval_jaxpr/psum | solution.py:12
  252.9 1.6 broadcast_select_fusion.8
  259.2 53.2 %all-reduce.2.cloned.1.call-done = bf16[1,1,128,2,128]{4,3,2,1,0:T(2,128)(2,1)} async-done(((bf16[1,1,128,2,128]{4,3,2,1,0:T(2,128)(2,1)}), bf16[1,1,128,2,128]{4,3,2,1,0:T(2,128)(2,1)}) %all-reduce.2.cloned.1.call-update) | async-done | bytes 65552 | tf_op jit(solution)/shard_map/while/body/eval_jaxpr/psum | solution.py:12
  312.4 1.6 broadcast_select_fusion.8
  318.7 53.2 %all-reduce.2.cloned.1.call-done = bf16[1,1,128,2,128]{4,3,2,1,0:T(2,128)(2,1)} async-done(((bf16[1,1,128,2,128]{4,3,2,1,0:T(2,128)(2,1)}), bf16[1,1,128,2,128]{4,3,2,1,0:T(2,128)(2,1)}) %all-reduce.2.cloned.1.call-update) | async-done | bytes 65552 | tf_op jit(solution)/shard_map/while/body/eval_jaxpr/psum | solution.py:12
  371.9 1.6 broadcast_select_fusion.8
  378.2 53.2 %all-reduce.2.cloned.1.call-done = bf16[1,1,128,2,128]{4,3,2,1,0:T(2,128)(2,1)} async-done(((bf16[1,1,128,2,128]{4,3,2,1,0:T(2,128)(2,1)}), bf16[1,1,128,2,128]{4,3,2,1,0:T(2,128)(2,1)}) %all-reduce.2.cloned.1.call-update) | async-done | bytes 65552 | tf_op jit(solution)/shard_map/while/body/eval_jaxpr/psum | solution.py:12
  431.4 1.6 broadcast_select_fusion.8
  437.7 53.2 %all-reduce.2.cloned.1.call-done = bf16[1,1,128,2,128]{4,3,2,1,0:T(2,128)(2,1)} async-done(((bf16[1,1,128,2,128]{4,3,2,1,0:T(2,128)(2,1)}), bf16[1,1,128,2,128]{4,3,2,1,0:T(2,128)(2,1)}) %all-reduce.2.cloned.1.call-update) | async-done | bytes 65552 | tf_op jit(solution)/shard_map/while/body/eval_jaxpr/psum | solution.py:12
  490.9 1.6 broadcast_select_fusion.8
  497.2 53.2 %all-reduce.2.cloned.1.call-done = bf16[1,1,128,2,128]{4,3,2,1,0:T(2,128)(2,1)} async-done(((bf16[1,1,128,2,128]{4,3,2,1,0:T(2,128)(2,1)}), bf16[1,1,128,2,128]{4,3,2,1,0:T(2,128)(2,1)}) %all-reduce.2.cloned.1.call-update) | async-done | bytes 65552 | tf_op jit(solution)/shard_map/while/body/eval_jaxpr/psum | solution.py:12
  550.4 1.6 broadcast_select_fusion.8
  556.7 53.2 %all-reduce.2.cloned.1.call-done = bf16[1,1,128,2,128]{4,3,2,1,0:T(2,128)(2,1)} async-done(((bf16[1,1,128,2,128]{4,3,2,1,0:T(2,128)(2,1)}), bf16[1,1,128,2,128]{4,3,2,1,0:T(2,128)(2,1)}) %all-reduce.2.cloned.1.call-update) | async-done | bytes 65552 | tf_op jit(solution)/shard_map/while/body/eval_jaxpr/psum | solution.py:12
  609.9 1.6 broadcast_select_fusion.8
  616.2 53.2 %all-reduce.2.cloned.1.call-done = bf16[1,1,128,2,128]{4,3,2,1,0:T(2,128)(2,1)} async-done(((bf16[1,1,128,2,128]{4,3,2,1,0:T(2,128)(2,1)}), bf16[1,1,128,2,128]{4,3,2,1,0:T(2,128)(2,1)}) %all-reduce.2.cloned.1.call-update) | async-done | bytes 65552 | tf_op jit(solution)/shard_map/while/body/eval_jaxpr/psum | solution.py:12
  669.4 1.6 broadcast_select_fusion.8
  675.7 53.2 %all-reduce.2.cloned.1.call-done = bf16[1,1,128,2,128]{4,3,2,1,0:T(2,128)(2,1)} async-done(((bf16[1,1,128,2,128]{4,3,2,1,0:T(2,128)(2,1)}), bf16[1,1,128,2,128]{4,3,2,1,0:T(2,128)(2,1)}) %all-reduce.2.cloned.1.call-update) | async-done | bytes 65552 | tf_op jit(solution)/shard_map/while/body/eval_jaxpr/psum | solution.py:12
  728.9 1.6 broadcast_select_fusion.8
  735.2 53.2 %all-reduce.2.cloned.1.call-done = bf16[1,1,128,2,128]{4,3,2,1,0:T(2,128)(2,1)} async-done(((bf16[1,1,128,2,128]{4,3,2,1,0:T(2,128)(2,1)}), bf16[1,1,128,2,128]{4,3,2,1,0:T(2,128)(2,1)}) %all-reduce.2.cloned.1.call-update) | async-done | bytes 65552 | tf_op jit(solution)/shard_map/while/body/eval_jaxpr/psum | solution.py:12
  788.4 1.6 broadcast_select_fusion.8
  794.7 53.2 %all-reduce.2.cloned.1.call-done = bf16[1,1,128,2,128]{4,3,2,1,0:T(2,128)(2,1)} async-done(((bf16[1,1,128,2,128]{4,3,2,1,0:T(2,128)(2,1)}), bf16[1,1,128,2,128]{4,3,2,1,0:T(2,128)(2,1)}) %all-reduce.2.cloned.1.call-update) | async-done | bytes 65552 | tf_op jit(solution)/shard_map/while/body/eval_jaxpr/psum | solution.py:12
  847.9 1.6 broadcast_select_fusion.8
  854.2 53.2 %all-reduce.2.cloned.1.call-done = bf16[1,1,128,2,128]{4,3,2,1,0:T(2,128)(2,1)} async-done(((bf16[1,1,128,2,128]{4,3,2,1,0:T(2,128)(2,1)}), bf16[1,1,128,2,128]{4,3,2,1,0:T(2,128)(2,1)}) %all-reduce.2.cloned.1.call-update) | async-done | bytes 65552 | tf_op jit(solution)/shard_map/while/body/eval_jaxpr/psum | solution.py:12
  907.4 1.6 broadcast_select_fusion.8
  913.7 53.2 %all-reduce.2.cloned.1.call-done = bf16[1,1,128,2,128]{4,3,2,1,0:T(2,128)(2,1)} async-done(((bf16[1,1,128,2,128]{4,3,2,1,0:T(2,128)(2,1)}), bf16[1,1,128,2,128]{4,3,2,1,0:T(2,128)(2,1)}) %all-reduce.2.cloned.1.call-update) | async-done | bytes 65552 | tf_op jit(solution)/shard_map/while/body/eval_jaxpr/psum | solution.py:12
  966.9 1.6 broadcast_select_fusion.8
  973.2 53.2 %all-reduce.2.cloned.1.call-done = bf16[1,1,128,2,128]{4,3,2,1,0:T(2,128)(2,1)} async-done(((bf16[1,1,128,2,128]{4,3,2,1,0:T(2,128)(2,1)}), bf16[1,1,128,2,128]{4,3,2,1,0:T(2,128)(2,1)}) %all-reduce.2.cloned.1.call-update) | async-done | bytes 65552 | tf_op jit(solution)/shard_map/while/body/eval_jaxpr/psum | solution.py:12
  1026.4 1.6 broadcast_select_fusion.8
  1032.7 53.2 %all-reduce.2.cloned.1.call-done = bf16[1,1,128,2,128]{4,3,2,1,0:T(2,128)(2,1)} async-done(((bf16[1,1,128,2,128]{4,3,2,1,0:T(2,128)(2,1)}), bf16[1,1,128,2,128]{4,3,2,1,0:T(2,128)(2,1)}) %all-reduce.2.cloned.1.call-update) | async-done | bytes 65552 | tf_op jit(solution)/shard_map/while/body/eval_jaxpr/psum | solution.py:12
  1085.9 1.6 broadcast_select_fusion.8
  1087.5 14.2 %while.31 = (s32[]{:T(128)}, bf16[2,128,1024]{2,1,0:T(8,128)(2,1)}, bf16[2,2,128,2,128]{4,2,1,3,0:T(8,128)(2,1)S(1)}, bf16[2,2,2,128,2,128]{5,3,2,1,4,0:T(8,128)...) while((s32[]{:T(128)}, bf16[2,128,1024]{2,1,0:T(8,128)(2,1)}, ...), condition=%wide.region_8.9_spmd.clone, body=%wide.region_4.8_spmd.clone.sunk | while | flops 757610624 | bytes 30544560 | solution.py:137
  1090.7 1.3 fusion.31
  1092.0 1.6 fusion.32
  1099.1 1.6 fusion.32
  (215 shorter events, 50.7 us)
Async XLA Ops:
  6.5 40.6 %all-gather.3.cloned.1.call-start = ((), (), s32[]{:S(2)}) async-start(), calls=%async_computation | async-start | bytes 2621440 | tf_op jit(solution)/shard_map/all_gather | solution.py:43
  7.3 55.1 %all-gather.5.cloned.1.call-start = ((), (), s32[]{:S(2)}) async-start(), calls=%async_computation.1 | async-start | bytes 6291456 | tf_op jit(solution)/shard_map/all_gather | solution.py:46
  66.4 4.4 copy-start.2
  66.8 33.4 %copy-start = (bf16[256,1024]{1,0:T(8,128)(2,1)S(1)}, bf16[256,1024]{1,0:T(8,128)(2,1)}, u32[]{:S(2)}) copy-start(bf16[256,1024]{1,0:T(8,128)(2,1)} %param.13) | copy-start | bytes 1572868
  68.7 3.7 collective-permute-start
  73.0 21.0 %collective-permute-start.1 = (bf16[2,2,2,128,2,128]{5,2,4,3,1,0:T(2,128)(2,1)S(1)}, bf16[2,2,2,128,2,128]{5,2,4,3,1,0:T(2,128)(2,1)S(1)}, u32[]{:S(2)}, u32[]{:S(2)}) collective-permute-start(bf16[2,2,2,128,2,128]{5,2,4,3,1,0:T(2,128)(2,1)S(1)} %broadcast_select_fusion.2), channel_id=1, source_target_pairs={{0,8},{4,12},{8,16},{12,20},{16,24},{20,28},{1,9},{5,13},{9,17},{1... | collective-permute-start | bytes 1572872 | tf_op jit(solution)/shard_map/ppermute | solution.py:18
  94.8 15.0 %collective-permute-start.2 = (bf16[2,2,2,128,2,128]{5,2,4,3,1,0:T(2,128)(2,1)S(1)}, bf16[2,2,2,128,2,128]{5,2,4,3,1,0:T(2,128)(2,1)S(1)}, u32[]{:S(2)}, u32[]{:S(2)}) collective-permute-start(bf16[2,2,2,128,2,128]{5,2,4,3,1,0:T(2,128)(2,1)S(1)} %broadcast_select_fusion.3), channel_id=1, source_target_pairs={{0,16},{4,20},{8,24},{12,28},{1,17},{5,21},{9,25},{13,29},{2,18},{... | collective-permute-start | bytes 1572872 | tf_op jit(solution)/shard_map/ppermute | solution.py:18
  109.8 6.5 copy-start.1
  109.8 6.5 copy-start.5
  110.4 3.1 collective-permute-start.3
  116.3 77.1 %all-reduce.2.cloned.1.call-start = ((), (), s32[]{:S(2)}) async-start(), calls=%async_computation.2 | async-start | bytes 131072 | tf_op jit(solution)/shard_map/while/body/eval_jaxpr/psum | solution.py:12
  195.0 57.9 %all-reduce.2.cloned.1.call-start = ((), (), s32[]{:S(2)}) async-start(), calls=%async_computation.2 | async-start | bytes 131072 | tf_op jit(solution)/shard_map/while/body/eval_jaxpr/psum | solution.py:12
  254.5 57.9 %all-reduce.2.cloned.1.call-start = ((), (), s32[]{:S(2)}) async-start(), calls=%async_computation.2 | async-start | bytes 131072 | tf_op jit(solution)/shard_map/while/body/eval_jaxpr/psum | solution.py:12
  314.0 57.9 %all-reduce.2.cloned.1.call-start = ((), (), s32[]{:S(2)}) async-start(), calls=%async_computation.2 | async-start | bytes 131072 | tf_op jit(solution)/shard_map/while/body/eval_jaxpr/psum | solution.py:12
  373.5 57.9 %all-reduce.2.cloned.1.call-start = ((), (), s32[]{:S(2)}) async-start(), calls=%async_computation.2 | async-start | bytes 131072 | tf_op jit(solution)/shard_map/while/body/eval_jaxpr/psum | solution.py:12
  433.0 57.9 %all-reduce.2.cloned.1.call-start = ((), (), s32[]{:S(2)}) async-start(), calls=%async_computation.2 | async-start | bytes 131072 | tf_op jit(solution)/shard_map/while/body/eval_jaxpr/psum | solution.py:12
  492.5 57.9 %all-reduce.2.cloned.1.call-start = ((), (), s32[]{:S(2)}) async-start(), calls=%async_computation.2 | async-start | bytes 131072 | tf_op jit(solution)/shard_map/while/body/eval_jaxpr/psum | solution.py:12
  552.0 57.9 %all-reduce.2.cloned.1.call-start = ((), (), s32[]{:S(2)}) async-start(), calls=%async_computation.2 | async-start | bytes 131072 | tf_op jit(solution)/shard_map/while/body/eval_jaxpr/psum | solution.py:12
  611.5 57.9 %all-reduce.2.cloned.1.call-start = ((), (), s32[]{:S(2)}) async-start(), calls=%async_computation.2 | async-start | bytes 131072 | tf_op jit(solution)/shard_map/while/body/eval_jaxpr/psum | solution.py:12
  671.0 57.9 %all-reduce.2.cloned.1.call-start = ((), (), s32[]{:S(2)}) async-start(), calls=%async_computation.2 | async-start | bytes 131072 | tf_op jit(solution)/shard_map/while/body/eval_jaxpr/psum | solution.py:12
  730.5 57.9 %all-reduce.2.cloned.1.call-start = ((), (), s32[]{:S(2)}) async-start(), calls=%async_computation.2 | async-start | bytes 131072 | tf_op jit(solution)/shard_map/while/body/eval_jaxpr/psum | solution.py:12
  790.0 57.9 %all-reduce.2.cloned.1.call-start = ((), (), s32[]{:S(2)}) async-start(), calls=%async_computation.2 | async-start | bytes 131072 | tf_op jit(solution)/shard_map/while/body/eval_jaxpr/psum | solution.py:12
  849.5 57.9 %all-reduce.2.cloned.1.call-start = ((), (), s32[]{:S(2)}) async-start(), calls=%async_computation.2 | async-start | bytes 131072 | tf_op jit(solution)/shard_map/while/body/eval_jaxpr/psum | solution.py:12
  909.0 57.9 %all-reduce.2.cloned.1.call-start = ((), (), s32[]{:S(2)}) async-start(), calls=%async_computation.2 | async-start | bytes 131072 | tf_op jit(solution)/shard_map/while/body/eval_jaxpr/psum | solution.py:12
  968.5 57.9 %all-reduce.2.cloned.1.call-start = ((), (), s32[]{:S(2)}) async-start(), calls=%async_computation.2 | async-start | bytes 131072 | tf_op jit(solution)/shard_map/while/body/eval_jaxpr/psum | solution.py:12
  1028.0 57.9 %all-reduce.2.cloned.1.call-start = ((), (), s32[]{:S(2)}) async-start(), calls=%async_computation.2 | async-start | bytes 131072 | tf_op jit(solution)/shard_map/while/body/eval_jaxpr/psum | solution.py:12
  1092.0 1.8 copy-start.3
  1093.8 0.8 copy-start.4
  1099.1 1.8 copy-start.3
  1100.9 0.8 copy-start.4
Sparse Core Ops, SparseCore 0:
  9.2 37.8 all-gather.2
  48.7 13.6 all-gather.4
  120.4 72.9 all-reduce.1
  199.1 53.7 all-reduce.1
  258.6 53.7 all-reduce.1
  318.1 53.7 all-reduce.1
  377.6 53.7 all-reduce.1
  437.1 53.7 all-reduce.1
  496.6 53.7 all-reduce.1
  556.1 53.7 all-reduce.1
  615.6 53.7 all-reduce.1
  675.1 53.7 all-reduce.1
  734.6 53.7 all-reduce.1
  794.1 53.7 all-reduce.1
  853.6 53.7 all-reduce.1
  913.1 53.7 all-reduce.1
  972.6 53.7 all-reduce.1
  1032.1 53.7 all-reduce.1
where the time goes:
time: 1110 us
  waiting for transfers between devices  947 us (85%)
  other arithmetic  53.8 us (5%)
  loops' own time  43 us (4%)
  starting transfers between devices  20.8 us (2%)
  local copies, waits for them, and re-layouts  19 us (2%)
  between operations  13.7 us (1%)
  matrix products  11.5 us (1%)
    psum x16, waiting for transfers between devices, broadcast(): return lax.psum(kept, axis)  870 us
    another operation x1, loops' own time, per_device(): lax.fori_loop(0, local_heads * vertical_count, fetch_block, start_buffer)  41.5 us
    all_gather x1, waiting for transfers between devices, per_device(): gathered = lax.all_gather(hidden, 'kvh', axis=1, tiled=True)  38.8 us
    another operation x33, other arithmetic  35.5 us
  transfers between devices with their start and end apart: 22, of which 21 were waited for; matrix products, arithmetic and copies ran while one was open for 1% of the time, Pallas kernels for 0%

commit v1 on v0

--- a/solution.py
+++ b/solution.py
@@ -9,7 +9,7 @@
 
 def broadcast(value, axis, source):
     kept = jnp.where(lax.axis_index(axis) == source, value, 0).astype(value.dtype)
-    return lax.psum(kept, axis)
+    return jnp.sum(lax.all_gather(kept, axis), axis=0)
 
 
 def from_behind(value, axis, by):

time: 1110 us -> 459 us (0.41)
  waiting for transfers between devices: 947 us -> 76.1 us
  blocking collectives: 0 us -> 251 us
  other arithmetic: 53.8 us -> 29 us
    psum x16 -> x0, waiting for transfers between devices: 870 us -> none  [broadcast(): return lax.psum(kept, axis)]
    all_gather x0 -> x16, blocking collectives: none -> 251 us  [broadcast(): return jnp.sum(lax.all_gather(kept, axis), axis=0)]
    another operation x33 -> x17, other arithmetic: 35.5 us -> 10.4 us
  transfers between devices with their start and end apart: 22 -> 6, of which waited for: 21 -> 5; matrix products, arithmetic and copies ran while one was open for 1% -> 8% of each run, Pallas kernels for 0% -> 0%
where the time goes in v1:
time: 459 us; the launch traced here: 458 us
  blocking collectives  251 us (55%)
  waiting for transfers between devices  76.1 us (17%)
  loops' own time  40 us (9%)
  other arithmetic  29 us (6%)
  starting transfers between devices  20.2 us (4%)
  local copies, waits for them, and re-layouts  17.4 us (4%)
  between operations  13.7 us (3%)
  matrix products  11.4 us (2%)
    all_gather x16, blocking collectives, broadcast(): return jnp.sum(lax.all_gather(kept, axis), axis=0)  251 us
    all_gather x1, waiting for transfers between devices, per_device(): gathered = lax.all_gather(hidden, 'kvh', axis=1, tiled=True)  38.8 us
    another operation x1, loops' own time, per_device(): lax.fori_loop(0, local_heads * vertical_count, fetch_block, start_buffer)  38.4 us
    ppermute x4, waiting for transfers between devices, from_behind(): return lax.ppermute(value, axis, pairs)  20.7 us
    ppermute x4, starting transfers between devices, from_behind(): return lax.ppermute(value, axis, pairs)  20.1 us
    all_gather x1, waiting for transfers between devices, per_device(): lax.all_gather(key_value_matrix, 'fsdp', axis=0, tiled=True)  15.2 us
    another operation x17, other arithmetic  10.4 us
    scatter x16, other arithmetic, fetch_block(): return buffer.at[head_index, slot_index].set(received)  9.73 us
  transfers between devices with their start and end apart: 6, of which 5 were waited for; matrix products, arithmetic and copies ran while one was open for 8% of the time, Pallas kernels for 0%

profile of v1, /device:TPU:0, one launch (start us, length us, event | category | flops | bytes accessed | tf_op | source)
XLA Modules:
  0.0 458.3 jit_solution(8719884779935344804)
XLA Ops:
  6.5 0.7 all-gather.6.cloned.1.call-update
  7.3 0.7 all-gather.8.cloned.1.call-update
  8.4 38.8 %all-gather.6.cloned.1.call-done = bf16[256,4096]{1,0:T(8,128)(2,1)} async-done(((bf16[256,1024]{1,0:T(8,128)(2,1)}), bf16[256,4096]{1,0:T(8,128)(2,1)}) %all-gather.6.cloned.1.call-update) | async-done | bytes 2097168 | tf_op jit(solution)/shard_map/all_gather | solution.py:43
  47.1 15.2 %all-gather.8.cloned.1.call-done = bf16[4096,512]{1,0:T(8,128)(2,1)} async-done(((bf16[2048,512]{1,0:T(8,128)(2,1)}), bf16[4096,512]{1,0:T(8,128)(2,1)}) %all-gather.8.cloned.1.call-update) | async-done | bytes 4194320 | tf_op jit(solution)/shard_map/all_gather | solution.py:46
  62.4 4.1 fusion.22
  68.7 2.2 collective-permute-start
  70.9 1.4 collective-permute-done
  72.4 0.7 broadcast_select_fusion
  73.0 10.5 %collective-permute-start.1 = (bf16[2,2,2,128,2,128]{5,2,4,3,1,0:T(2,128)(2,1)S(1)}, bf16[2,2,2,128,2,128]{5,2,4,3,1,0:T(2,128)(2,1)S(1)}, u32[]{:S(2)}, u32[]{:S(2)}) collective-permute-start(bf16[2,2,2,128,2,128]{5,2,4,3,1,0:T(2,128)(2,1)S(1)} %broadcast_select_fusion), channel_id=1, source_target_pairs={{0,8},{4,12},{8,16},{12,20},{16,24},{20,28},{1,9},{5,13},{9,17},{1... | collective-permute-start | bytes 1572872 | tf_op jit(solution)/shard_map/ppermute | solution.py:18
  84.0 10.0 %collective-permute-done.1 = bf16[2,2,2,128,2,128]{5,2,4,3,1,0:T(2,128)(2,1)S(1)} collective-permute-done((bf16[2,2,2,128,2,128]{5,2,4,3,1,0:T(2,128)(2,1)S(1)}, bf16[2,2,2,128,2,128]{5,2,4,3,1,0:T(2,128)(2,1)S(1)}, u32[]{:S(2)}, u32[]{:S(2)}) %collective-permute-start.1) | collective-permute-done | bytes 524320 | tf_op jit(solution)/shard_map/ppermute | solution.py:18
  94.0 0.8 broadcast_select_fusion.1
  94.8 5.3 %collective-permute-start.2 = (bf16[2,2,2,128,2,128]{5,2,4,3,1,0:T(2,128)(2,1)S(1)}, bf16[2,2,2,128,2,128]{5,2,4,3,1,0:T(2,128)(2,1)S(1)}, u32[]{:S(2)}, u32[]{:S(2)}) collective-permute-start(bf16[2,2,2,128,2,128]{5,2,4,3,1,0:T(2,128)(2,1)S(1)} %broadcast_select_fusion.1), channel_id=1, source_target_pairs={{0,16},{4,20},{8,24},{12,28},{1,17},{5,21},{9,25},{13,29},{2,18},{... | collective-permute-start | bytes 1572872 | tf_op jit(solution)/shard_map/ppermute | solution.py:18
  100.4 9.3 %collective-permute-done.2 = bf16[2,2,2,128,2,128]{5,2,4,3,1,0:T(2,128)(2,1)S(1)} collective-permute-done((bf16[2,2,2,128,2,128]{5,2,4,3,1,0:T(2,128)(2,1)S(1)}, bf16[2,2,2,128,2,128]{5,2,4,3,1,0:T(2,128)(2,1)S(1)}, u32[]{:S(2)}, u32[]{:S(2)}) %collective-permute-start.2) | collective-permute-done | bytes 524320 | tf_op jit(solution)/shard_map/ppermute | solution.py:18
  110.4 2.1 collective-permute-start.3
  112.7 321.6 %while.30 = (s32[]{:T(128)}, bf16[2,8,128,2,128]{4,2,1,0,3:T(8,128)(2,1)S(1)}, s32[2,8]{1,0:T(2,128)S(1)}, bf16[2,2,128,2,128]{4,2,3,1,0:T(8,128)(2,1)S(1)}, s32...) while((s32[]{:T(128)}, ...), condition=%wide.region_3.4_spmd, body=%wide.region_0.3_spmd.sunk | while | flops 294984 | bytes 1639211 | solution.py:73
  115.7 24.6 %all-gather.2 = bf16[8,1,128,2,128]{4,2,3,1,0:T(8,128)(2,1)S(1)} all-gather(bf16[1,1,128,2,128]{4,2,3,1,0:T(8,128)(2,1)S(1)} %dynamic-slice_select_fusion.2), channel_id=2, replica_groups=mesh['ctx'=4,'fsdp'=2,'kvh'=4] {'ctx','fsdp'}, dimensions={0}, use_global_device_ids=true | all-gather | bytes 589824 | tf_op jit(solution)/shard_map/while/body/eval_jaxpr/all_gather | solution.py:12
  140.5 0.6 and_reduce_fusion.2
  144.8 14.8 %all-gather.2 = bf16[8,1,128,2,128]{4,2,3,1,0:T(8,128)(2,1)S(1)} all-gather(bf16[1,1,128,2,128]{4,2,3,1,0:T(8,128)(2,1)S(1)} %dynamic-slice_select_fusion.2), channel_id=2, replica_groups=mesh['ctx'=4,'fsdp'=2,'kvh'=4] {'ctx','fsdp'}, dimensions={0}, use_global_device_ids=true | all-gather | bytes 589824 | tf_op jit(solution)/shard_map/while/body/eval_jaxpr/all_gather | solution.py:12
  164.0 15.1 %all-gather.2 = bf16[8,1,128,2,128]{4,2,3,1,0:T(8,128)(2,1)S(1)} all-gather(bf16[1,1,128,2,128]{4,2,3,1,0:T(8,128)(2,1)S(1)} %dynamic-slice_select_fusion.2), channel_id=2, replica_groups=mesh['ctx'=4,'fsdp'=2,'kvh'=4] {'ctx','fsdp'}, dimensions={0}, use_global_device_ids=true | all-gather | bytes 589824 | tf_op jit(solution)/shard_map/while/body/eval_jaxpr/all_gather | solution.py:12
  179.3 0.6 and_reduce_fusion.2
  183.5 15.1 %all-gather.2 = bf16[8,1,128,2,128]{4,2,3,1,0:T(8,128)(2,1)S(1)} all-gather(bf16[1,1,128,2,128]{4,2,3,1,0:T(8,128)(2,1)S(1)} %dynamic-slice_select_fusion.2), channel_id=2, replica_groups=mesh['ctx'=4,'fsdp'=2,'kvh'=4] {'ctx','fsdp'}, dimensions={0}, use_global_device_ids=true | all-gather | bytes 589824 | tf_op jit(solution)/shard_map/while/body/eval_jaxpr/all_gather | solution.py:12
  198.8 0.6 and_reduce_fusion.2
  203.1 15.1 %all-gather.2 = bf16[8,1,128,2,128]{4,2,3,1,0:T(8,128)(2,1)S(1)} all-gather(bf16[1,1,128,2,128]{4,2,3,1,0:T(8,128)(2,1)S(1)} %dynamic-slice_select_fusion.2), channel_id=2, replica_groups=mesh['ctx'=4,'fsdp'=2,'kvh'=4] {'ctx','fsdp'}, dimensions={0}, use_global_device_ids=true | all-gather | bytes 589824 | tf_op jit(solution)/shard_map/while/body/eval_jaxpr/all_gather | solution.py:12
  218.3 0.6 and_reduce_fusion.2
  222.6 15.1 %all-gather.2 = bf16[8,1,128,2,128]{4,2,3,1,0:T(8,128)(2,1)S(1)} all-gather(bf16[1,1,128,2,128]{4,2,3,1,0:T(8,128)(2,1)S(1)} %dynamic-slice_select_fusion.2), channel_id=2, replica_groups=mesh['ctx'=4,'fsdp'=2,'kvh'=4] {'ctx','fsdp'}, dimensions={0}, use_global_device_ids=true | all-gather | bytes 589824 | tf_op jit(solution)/shard_map/while/body/eval_jaxpr/all_gather | solution.py:12
  237.8 0.6 and_reduce_fusion.2
  242.1 15.1 %all-gather.2 = bf16[8,1,128,2,128]{4,2,3,1,0:T(8,128)(2,1)S(1)} all-gather(bf16[1,1,128,2,128]{4,2,3,1,0:T(8,128)(2,1)S(1)} %dynamic-slice_select_fusion.2), channel_id=2, replica_groups=mesh['ctx'=4,'fsdp'=2,'kvh'=4] {'ctx','fsdp'}, dimensions={0}, use_global_device_ids=true | all-gather | bytes 589824 | tf_op jit(solution)/shard_map/while/body/eval_jaxpr/all_gather | solution.py:12
  261.6 15.1 %all-gather.2 = bf16[8,1,128,2,128]{4,2,3,1,0:T(8,128)(2,1)S(1)} all-gather(bf16[1,1,128,2,128]{4,2,3,1,0:T(8,128)(2,1)S(1)} %dynamic-slice_select_fusion.2), channel_id=2, replica_groups=mesh['ctx'=4,'fsdp'=2,'kvh'=4] {'ctx','fsdp'}, dimensions={0}, use_global_device_ids=true | all-gather | bytes 589824 | tf_op jit(solution)/shard_map/while/body/eval_jaxpr/all_gather | solution.py:12
  281.2 15.1 %all-gather.2 = bf16[8,1,128,2,128]{4,2,3,1,0:T(8,128)(2,1)S(1)} all-gather(bf16[1,1,128,2,128]{4,2,3,1,0:T(8,128)(2,1)S(1)} %dynamic-slice_select_fusion.2), channel_id=2, replica_groups=mesh['ctx'=4,'fsdp'=2,'kvh'=4] {'ctx','fsdp'}, dimensions={0}, use_global_device_ids=true | all-gather | bytes 589824 | tf_op jit(solution)/shard_map/while/body/eval_jaxpr/all_gather | solution.py:12
  300.7 15.1 %all-gather.2 = bf16[8,1,128,2,128]{4,2,3,1,0:T(8,128)(2,1)S(1)} all-gather(bf16[1,1,128,2,128]{4,2,3,1,0:T(8,128)(2,1)S(1)} %dynamic-slice_select_fusion.2), channel_id=2, replica_groups=mesh['ctx'=4,'fsdp'=2,'kvh'=4] {'ctx','fsdp'}, dimensions={0}, use_global_device_ids=true | all-gather | bytes 589824 | tf_op jit(solution)/shard_map/while/body/eval_jaxpr/all_gather | solution.py:12
  320.2 15.1 %all-gather.2 = bf16[8,1,128,2,128]{4,2,3,1,0:T(8,128)(2,1)S(1)} all-gather(bf16[1,1,128,2,128]{4,2,3,1,0:T(8,128)(2,1)S(1)} %dynamic-slice_select_fusion.2), channel_id=2, replica_groups=mesh['ctx'=4,'fsdp'=2,'kvh'=4] {'ctx','fsdp'}, dimensions={0}, use_global_device_ids=true | all-gather | bytes 589824 | tf_op jit(solution)/shard_map/while/body/eval_jaxpr/all_gather | solution.py:12
  339.7 15.1 %all-gather.2 = bf16[8,1,128,2,128]{4,2,3,1,0:T(8,128)(2,1)S(1)} all-gather(bf16[1,1,128,2,128]{4,2,3,1,0:T(8,128)(2,1)S(1)} %dynamic-slice_select_fusion.2), channel_id=2, replica_groups=mesh['ctx'=4,'fsdp'=2,'kvh'=4] {'ctx','fsdp'}, dimensions={0}, use_global_device_ids=true | all-gather | bytes 589824 | tf_op jit(solution)/shard_map/while/body/eval_jaxpr/all_gather | solution.py:12
  359.2 15.1 %all-gather.2 = bf16[8,1,128,2,128]{4,2,3,1,0:T(8,128)(2,1)S(1)} all-gather(bf16[1,1,128,2,128]{4,2,3,1,0:T(8,128)(2,1)S(1)} %dynamic-slice_select_fusion.2), channel_id=2, replica_groups=mesh['ctx'=4,'fsdp'=2,'kvh'=4] {'ctx','fsdp'}, dimensions={0}, use_global_device_ids=true | all-gather | bytes 589824 | tf_op jit(solution)/shard_map/while/body/eval_jaxpr/all_gather | solution.py:12
  378.8 15.1 %all-gather.2 = bf16[8,1,128,2,128]{4,2,3,1,0:T(8,128)(2,1)S(1)} all-gather(bf16[1,1,128,2,128]{4,2,3,1,0:T(8,128)(2,1)S(1)} %dynamic-slice_select_fusion.2), channel_id=2, replica_groups=mesh['ctx'=4,'fsdp'=2,'kvh'=4] {'ctx','fsdp'}, dimensions={0}, use_global_device_ids=true | all-gather | bytes 589824 | tf_op jit(solution)/shard_map/while/body/eval_jaxpr/all_gather | solution.py:12
  398.3 15.1 %all-gather.2 = bf16[8,1,128,2,128]{4,2,3,1,0:T(8,128)(2,1)S(1)} all-gather(bf16[1,1,128,2,128]{4,2,3,1,0:T(8,128)(2,1)S(1)} %dynamic-slice_select_fusion.2), channel_id=2, replica_groups=mesh['ctx'=4,'fsdp'=2,'kvh'=4] {'ctx','fsdp'}, dimensions={0}, use_global_device_ids=true | all-gather | bytes 589824 | tf_op jit(solution)/shard_map/while/body/eval_jaxpr/all_gather | solution.py:12
  417.8 15.1 %all-gather.2 = bf16[8,1,128,2,128]{4,2,3,1,0:T(8,128)(2,1)S(1)} all-gather(bf16[1,1,128,2,128]{4,2,3,1,0:T(8,128)(2,1)S(1)} %dynamic-slice_select_fusion.2), channel_id=2, replica_groups=mesh['ctx'=4,'fsdp'=2,'kvh'=4] {'ctx','fsdp'}, dimensions={0}, use_global_device_ids=true | all-gather | bytes 589824 | tf_op jit(solution)/shard_map/while/body/eval_jaxpr/all_gather | solution.py:12
  435.0 2.3 fusion.10
  437.3 14.1 %while.31 = (s32[]{:T(128)}, bf16[2,128,1024]{2,1,0:T(8,128)(2,1)}, bf16[2,2,128,2,128]{4,2,1,3,0:T(8,128)(2,1)S(1)}, bf16[2,2,2,128,2,128]{5,3,2,1,4,0:T(8,128)...) while((s32[]{:T(128)}, bf16[2,128,1024]{2,1,0:T(8,128)(2,1)}, ...), condition=%wide.region_8.9_spmd.clone, body=%wide.region_4.8_spmd.clone.sunk | while | flops 757610624 | bytes 26350708 | solution.py:137
  437.4 0.7 dynamic_slice.64
  439.7 0.9 fusion.30
  440.6 1.3 fusion.31
  441.9 1.6 fusion.32
  443.7 0.7 constant_dynamic-update-slice_fusion.2
  444.4 0.7 dynamic_slice.64
  446.7 0.9 fusion.30
  447.7 1.3 fusion.31
  449.0 1.6 fusion.32
  450.7 0.7 constant_dynamic-update-slice_fusion.2
  (175 shorter events, 36.3 us)
Async XLA Ops:
  6.5 40.6 %all-gather.6.cloned.1.call-start = ((), (), s32[]{:S(2)}) async-start(), calls=%async_computation | async-start | bytes 2621440 | tf_op jit(solution)/shard_map/all_gather | solution.py:43
  7.3 55.1 %all-gather.8.cloned.1.call-start = ((), (), s32[]{:S(2)}) async-start(), calls=%async_computation.1 | async-start | bytes 6291456 | tf_op jit(solution)/shard_map/all_gather | solution.py:46
  66.4 4.5 copy-start.2
  66.4 17.2 %copy-start = (bf16[256,1024]{1,0:T(8,128)(2,1)S(1)}, bf16[256,1024]{1,0:T(8,128)(2,1)}, u32[]{:S(2)}) copy-start(bf16[256,1024]{1,0:T(8,128)(2,1)} %param.13) | copy-start | bytes 1572868
  68.4 44.3 %copy-start.1 = (s32[2,8]{1,0:T(2,128)S(1)}, s32[2,8]{1,0:T(2,128)}, u32[]{:S(2)}) copy-start(s32[2,8]{1,0:T(2,128)} %param.14) | copy-start | bytes 196
  68.4 44.3 %copy-start.3 = (s32[5]{0:T(128)S(1)}, s32[5]{0:T(128)}, u32[]{:S(2)}) copy-start(s32[5]{0:T(128)} %constant.409.clone.1) | copy-start | bytes 64
  68.7 3.7 collective-permute-start
  73.0 21.0 %collective-permute-start.1 = (bf16[2,2,2,128,2,128]{5,2,4,3,1,0:T(2,128)(2,1)S(1)}, bf16[2,2,2,128,2,128]{5,2,4,3,1,0:T(2,128)(2,1)S(1)}, u32[]{:S(2)}, u32[]{:S(2)}) collective-permute-start(bf16[2,2,2,128,2,128]{5,2,4,3,1,0:T(2,128)(2,1)S(1)} %broadcast_select_fusion), channel_id=1, source_target_pairs={{0,8},{4,12},{8,16},{12,20},{16,24},{20,28},{1,9},{5,13},{9,17},{1... | collective-permute-start | bytes 1572872 | tf_op jit(solution)/shard_map/ppermute | solution.py:18
  94.8 15.0 %collective-permute-start.2 = (bf16[2,2,2,128,2,128]{5,2,4,3,1,0:T(2,128)(2,1)S(1)}, bf16[2,2,2,128,2,128]{5,2,4,3,1,0:T(2,128)(2,1)S(1)}, u32[]{:S(2)}, u32[]{:S(2)}) collective-permute-start(bf16[2,2,2,128,2,128]{5,2,4,3,1,0:T(2,128)(2,1)S(1)} %broadcast_select_fusion.1), channel_id=1, source_target_pairs={{0,16},{4,20},{8,24},{12,28},{1,17},{5,21},{9,25},{13,29},{2,18},{... | collective-permute-start | bytes 1572872 | tf_op jit(solution)/shard_map/ppermute | solution.py:18
  110.4 324.6 %collective-permute-start.3 = (bf16[2,2,2,128,2,128]{5,2,4,3,1,0:T(2,128)(2,1)S(1)}, bf16[2,2,2,128,2,128]{5,2,4,3,1,0:T(2,128)(2,1)}, u32[]{:S(2)}, u32[]{:S(2)}) collective-permute-start(bf16[2,2,2,128,2,128]{5,2,4,3,1,0:T(2,128)(2,1)S(1)} %broadcast_select_fusion.2), channel_id=1, source_target_pairs={{0,4},{4,8},{8,12},{12,16},{16,20},{20,24},{24,28},{1,5},{5,9},{9,... | collective-permute-start | bytes 1572872 | tf_op jit(solution)/shard_map/ppermute | solution.py:18
Sparse Core Ops, SparseCore 0:
  9.2 37.8 all-gather.5
  48.7 13.6 all-gather.7
